TPU v7x, 256 devices: a whole 4x4x8 slice. The times are simulated.
256 devices in a mesh: row: 64 (over x, z, core), col: 4 (over y).
Axes of the slice: x: 4, y: 4, z: 8, core: 2. Of those that a mesh axis runs over, the one named last changes fastest.
Arguments:
- matrix: float32 [128, 4194304], P('col', 'row'), may hold values from -200 to 200
- row_signs: int32 [4194304], P('row'), may hold values from -1 to 1, as said below
- sample_rows: int32 [2048], replicated, may hold values from 0 to 4194303, as said below
- target: float32 [4194304], P('row'), may hold values from -6 to 6
Outputs:
- gradient: float32 [128], replicated
- residual: float32 [4194304], P('row')
Inputs may be any that keep to these rules, and one draw needn't show every extreme that they name: `row_signs`: each entry is -1 or +1. `sample_rows`: indices may repeat; 0 and 4194303 are always among them.
All inputs are finite; a program needn't handle non-finite values.
Results may differ from a plain program's by a relative error of at most 0.0003.
Values sent between devices are 32-bit elements; how exact they have to be, the bound alone decides.
No kernel may reach another device: no remote copies, remote signals or barrier semaphores. Data moves between devices by JAX's collectives and lax.ppermute only.
A program may use at most 128 MiB of HBM per device.

v0:
```python
import jax
import jax.numpy as jnp
from jax import lax
from jax.sharding import PartitionSpec as P


def walsh_transform(order):
    index = jnp.arange(order, dtype=jnp.int32)
    common = jnp.bitwise_and(index[:, None], index[None, :])
    parity = jnp.zeros((order, order), jnp.int32)
    for shift in range(max(order.bit_length() - 1, 1)):
        parity = parity + jnp.bitwise_and(jnp.right_shift(common, shift), 1)
    return (1 - 2 * (parity % 2)).astype(jnp.float32)


def body(matrix, row_signs, sample_rows, target):
    upper_limit = lax.Precision.HIGHEST
    cols_dev, rows_dev = matrix.shape
    row_count = lax.axis_size("row")
    my_index = lax.axis_index("row")
    total_rows = rows_dev * row_count
    slice_len = rows_dev // row_count
    inv_root = 1.0 / jnp.sqrt(jnp.float32(total_rows))
    signed = matrix * row_signs.astype(jnp.float32)[None, :]
    block_list = signed.reshape(cols_dev, rows_dev // 128, 128)
    block_list = jnp.einsum("cbt,ts->cbs", block_list, walsh_transform(128), precision=upper_limit)
    block_list = jnp.einsum(
        "cbs,ba->cas", block_list, walsh_transform(rows_dev // 128), precision=upper_limit
    )
    spread = block_list.reshape(cols_dev, row_count, slice_len)
    arrived = lax.all_to_all(spread, "row", split_axis=1, concat_axis=1, tiled=True)
    mixed = jnp.einsum("cpj,pk->ckj", arrived, walsh_transform(row_count), precision=upper_limit)
    mixed = mixed * inv_root
    local_rows = lax.all_to_all(mixed, "row", split_axis=1, concat_axis=1, tiled=True).reshape(
        cols_dev, rows_dev
    )
    owner_dev = sample_rows // rows_dev
    where_at = sample_rows % rows_dev
    chosen = jnp.where(
        (owner_dev == my_index)[None, :], jnp.take(local_rows, where_at, axis=1), 0.0
    )
    rhs_part = jnp.dot(matrix, target, precision=upper_limit)
    weight = total_rows / sample_rows.shape[0]
    selected_row_sum, rhs_sum = lax.psum((chosen, rhs_part), "row")
    whole_cols, rhs_all = (
        lax.all_gather(selected_row_sum, "col", axis=0, tiled=True),
        lax.all_gather(rhs_sum, "col", axis=0, tiled=True),
    )
    cross_product_matrix = jnp.dot(whole_cols, whole_cols.T, precision=upper_limit) * weight
    lower = jnp.linalg.cholesky(cross_product_matrix)
    gradient = lax.linalg.triangular_solve(lower, rhs_all[:, None], left_side=True, lower=True)[
        :, 0
    ]
    estimate = lax.linalg.triangular_solve(
        lower, gradient[:, None], left_side=True, lower=True, transpose_a=True
    )[:, 0]
    col_index = lax.axis_index("col")
    local_estimate = lax.dynamic_slice_in_dim(estimate, col_index * cols_dev, cols_dev, 0)
    fitted_portion = jnp.dot(local_estimate, matrix, precision=upper_limit)
    fitted = lax.psum(fitted_portion, "col")
    return (gradient, target - fitted)


def solution(mesh):
    return jax.shard_map(
        body,
        mesh=mesh,
        in_specs=(P("col", "row"), P("row"), P(), P("row")),
        out_specs=(P(), P("row")),
        check_vma=False,
    )
```

profile of v0, /device:TPU:2, one launch (start us, length us, event | category | flops | bytes accessed | tf_op | source)
XLA Modules:
  0.0 919.7 jit_solution(17685823326387873341)
XLA Ops:
  7.2 1.0 convert_element_type.14
  8.1 4.1 multiply_bitcast_fusion.1
  12.3 1.5 copy.14
  13.7 8.6 fusion.28
  22.3 18.4 %convolution_bitcast_fusion = f32[32,512,128]{2,1,0:T(8,128)} fusion(f32[32,512,128]{2,1,0:T(8,128)S(1)} %fusion.28), kind=kOutput, calls=%fused_computation.5 | convolution fusion | flops 12895649792 | bytes 16777216 | tf_op jit(solution)/shard_map/cbs,ba->cas/dot_general | solution.py:27
  40.7 9.4 %reshape.41 = f32[32,64,1024]{2,1,0:T(8,128)} reshape(f32[32,512,128]{2,1,0:T(8,128)} %convolution_bitcast_fusion) | data formatting | bytes 16777216 | tf_op jit(solution)/shard_map/reshape | solution.py:30
  50.1 8.2 copy.8
  58.4 196.0 %all_to_all.10 = f32[32,64,1024]{2,0,1:T(8,128)S(1)} all-to-all(f32[32,64,1024]{2,0,1:T(8,128)S(1)} %copy.8), channel_id=1, replica_groups=mesh['row'=64,'col'=4] {'row'}, dimensions={1} | all-to-all | bytes 16777216 | tf_op jit(solution)/shard_map/all_to_all | solution.py:31
  254.3 12.5 %multiply_bitcast_fusion = f32[32,64,1024]{2,1,0:T(8,128)S(1)} fusion(f32[32,64,1024]{2,0,1:T(8,128)S(1)} %all_to_all.10), kind=kOutput, calls=%fused_computation.3 | convolution fusion | flops 1612840960 | bytes 16777216 | tf_op jit(solution)/shard_map/cpj,pk->ckj/dot_general | solution.py:32
  266.8 8.5 copy.10
  275.3 8.1 all-to-all-start.1
  283.5 184.1 %all-to-all-done.1 = f32[32,64,1024]{2,0,1:T(8,128)} async-done(((f32[32,64,1024]{2,0,1:T(8,128)}), f32[32,64,1024]{2,0,1:T(8,128)}, u32[]{:S(2)}, u32[]{:S(2)}) %all-to-all-start.1) | async-done | bytes 8388640 | tf_op jit(solution)/shard_map/all_to_all | solution.py:34
  467.6 19.6 %copy.11 = f32[32,64,1024]{0,2,1:T(8,128)} copy(f32[32,64,1024]{2,0,1:T(8,128)} %all-to-all-done.1) | data formatting | bytes 16777216 | tf_op jit(solution)/shard_map/all_to_all | solution.py:34
  487.2 16.0 %gather_fusion = f32[2048,32]{1,0:T(8,128)S(1)} fusion(f32[32,65536]{0,1:T(8,128)} %bitcast.55, s32[2048]{0:T(1024)S(1)} %broadcast_clamp_fusion), kind=kCustom, calls=%fused_computation | custom fusion | bytes 532480 | tf_op jit(solution)/shard_map/jit(_take)/gather | solution.py:40
  503.2 2.4 select_bitcast_fusion
  505.7 185.2 %all-reduce.4.cloned.1.call-done = f32[32,2048]{0,1:T(8,128)} async-done(((f32[32,2048]{0,1:T(8,128)}), f32[32,2048]{0,1:T(8,128)}) %all-reduce.4.cloned.1.call-update) | async-done | bytes 262160 | tf_op jit(solution)/shard_map/psum | solution.py:44
  690.9 2.2 copy.12
  693.3 0.6 dynamic-slice.1
  694.5 8.9 convolution_bitcast_fusion.1
  703.4 104.7 %psum.22 = f32[32]{0:T(128)S(1)} all-reduce(f32[32]{0:T(128)S(1)} %convolution_bitcast_fusion.1), channel_id=1, replica_groups=mesh['row'=64,'col'=4] {'row'}, use_global_device_ids=true, to_apply=%region_3.4 | all-reduce | flops 32 | bytes 256 | tf_op jit(solution)/shard_map/psum | solution.py:44
  808.1 0.2 dynamic-update-slice.3
  808.3 10.7 %all-reduce = f32[128]{0:T(128)S(1)} all-reduce(f32[128]{0:T(128)S(1)} %dynamic-update-slice.3), channel_id=1, replica_groups=mesh['row'=64,'col'=4] {'col'}, use_global_device_ids=true, to_apply=%add | all-reduce | flops 128 | bytes 1024
  819.1 2.5 fusion.89
  821.7 11.7 %cholesky.16 = f32[128,128]{1,0:T(8,128)S(1)} custom-call(f32[128,128]{1,0:T(8,128)S(1)} %fusion.33), custom_call_target="Cholesky" | custom-call | tf_op jit(solution)/shard_map/jit(cholesky)/cholesky | solution.py:50
  833.5 0.6 compare_reduce_fusion
  834.1 0.7 fusion.22
  834.8 9.8 %custom-call.8 = f32[1,128,128]{1,2,0:T(8,128)S(1)} custom-call(f32[1,128,128]{2,1,0:T(8,128)S(1)} %fusion.22), custom_call_target="InvertDiagBlocksLowerTriangular" | custom-call | tf_op jit(solution)/shard_map/triangular_solve | solution.py:51
  844.6 0.2 fusion.31
  844.7 0.2 convolution_bitcast_fusion.2
  844.9 7.1 fusion.62
  852.0 59.2 %all-reduce.6.cloned.1.call-done = f32[65536]{0:T(1024)} async-done(((f32[65536]{0:T(1024)}), f32[65536]{0:T(1024)}) %all-reduce.6.cloned.1.call-update) | async-done | bytes 262160 | tf_op jit(solution)/shard_map/psum | solution.py:60
  911.3 1.7 sub.22
  (21 shorter events, 0.4 us)
Async XLA Ops:
  275.3 8.1 copy-start.1
  275.3 192.3 %all-to-all-start.1 = ((f32[32,64,1024]{2,0,1:T(8,128)}), f32[32,64,1024]{2,0,1:T(8,128)}, u32[]{:S(2)}, u32[]{:S(2)}) async-start(f32[32,64,1024]{2,0,1:T(8,128)} %copy.10), calls=%async_computation.1 | async-start | bytes 16777216 | tf_op jit(solution)/shard_map/all_to_all | solution.py:34
  283.3 407.6 %all-reduce.4.cloned.1.call-start = ((), (), s32[]{:S(2)}) async-start(), calls=%async_computation.2 | async-start | bytes 2097152 | tf_op jit(solution)/shard_map/psum | solution.py:44
  283.5 409.8 %copy-start.3 = (u32[256]{0:T(256)S(1)}, u32[256]{0:T(256)}, u32[]{:S(2)}) copy-start(u32[256]{0:T(256)} %constant.164) | copy-start | bytes 3076
  283.5 411.0 %copy-start = (f32[65536]{0:T(1024)S(1)}, f32[65536]{0:T(1024)}, u32[]{:S(2)}) copy-start(f32[65536]{0:T(1024)} %param.7) | copy-start | bytes 786436
  505.7 313.4 %all-gather.2.cloned.1.call-start = ((), (), s32[]{:S(2)}) async-start(), calls=%async_computation.3 | async-start | bytes 1310720 | tf_op jit(solution)/shard_map/all_gather | solution.py:46
  693.2 218.1 %all-reduce.6.cloned.1.call-start = ((), (), s32[]{:S(2)}) async-start(), calls=%async_computation.4 | async-start | bytes 524288 | tf_op jit(solution)/shard_map/psum | solution.py:60
  844.7 68.2 %copy-start.2 = (f32[1,128]{1,0:T(1,128)}, f32[1,128]{1,0:T(1,128)S(1)}, u32[]{:S(2)}) copy-start(f32[1,128]{1,0:T(1,128)S(1)} %fusion.31) | copy-start | bytes 1540
Sparse Core Ops, SparseCore 0:
  505.8 185.1 all-reduce.3
  693.3 23.8 all-gather.1
  852.1 59.0 all-reduce.5
where the time goes:
time: 923 us; the launch traced here: 920 us
  waiting for transfers between devices  429 us (46%)
  blocking collectives  311 us (34%)
  local copies, waits for them, and re-layouts  66.4 us (7%)
  matrix products  58.3 us (6%)
  other arithmetic  32.1 us (3%)
  between operations  14.8 us (2%)
    all_to_all x1, blocking collectives, body(): lax.all_to_all(spread, 'row', split_axis=1, concat_axis=1, tiled=True)  196 us
    psum x1, waiting for transfers between devices, body(): selected_row_sum, rhs_sum = lax.psum((chosen, rhs_part), 'row')  185 us
    all_to_all x1, waiting for transfers between devices, body(): lax.all_to_all(mixed, 'row', split_axis=1, concat_axis=1, tiled=True)  184 us
    psum x1, blocking collectives, body(): selected_row_sum, rhs_sum = lax.psum((chosen, rhs_part), 'row')  105 us
    psum x1, waiting for transfers between devices, body(): fitted = lax.psum(fitted_portion, 'col')  59.2 us
    all_to_all x1, local copies, waits for them, and re-layouts, body(): lax.all_to_all(mixed, 'row', split_axis=1, concat_axis=1, tiled=True)  19.6 us
  transfers between devices with their start and end apart: 4, of which 3 were waited for; matrix products, arithmetic and copies ran while one was open for 1% of the time, Pallas kernels for 0%

commit v1 on v0

--- a/solution.py
+++ b/solution.py
@@ -28,7 +28,10 @@
         "cbs,ba->cas", block_list, walsh_transform(rows_dev // 128), precision=upper_limit
     )
     spread = block_list.reshape(cols_dev, row_count, slice_len)
-    arrived = lax.all_to_all(spread, "row", split_axis=1, concat_axis=1, tiled=True)
+    arrived = jnp.concatenate(
+        lax.all_to_all(jnp.stack(jnp.split(spread, lax.axis_size("row"), axis=1)), "row", 0, 0),
+        axis=1,
+    )
     mixed = jnp.einsum("cpj,pk->ckj", arrived, walsh_transform(row_count), precision=upper_limit)
     mixed = mixed * inv_root
     local_rows = lax.all_to_all(mixed, "row", split_axis=1, concat_axis=1, tiled=True).reshape(

time: 923 us -> 950 us (1.029)
  local copies, waits for them, and re-layouts: 66.4 us -> 92.8 us
    split x0 -> x4, local copies, waits for them, and re-layouts: none -> 33 us  [body(): jnp.split(spread, lax.axis_size('row'), axis=1)]
where the time goes in v1:
time: 950 us; the launch traced here: 947 us
  waiting for transfers between devices  429 us (45%)
  blocking collectives  311 us (33%)
  local copies, waits for them, and re-layouts  92.8 us (10%)
  matrix products  58.3 us (6%)
  other arithmetic  32.1 us (3%)
  between operations  15.3 us (2%)
    all_to_all x1, blocking collectives, body(): lax.all_to_all(jnp.stack(jnp.split(spread, lax.axis_size('row'), axis=1))...  196 us
    psum x1, waiting for transfers between devices, body(): selected_row_sum, rhs_sum = lax.psum((chosen, rhs_part), 'row')  185 us
    all_to_all x1, waiting for transfers between devices, body(): lax.all_to_all(mixed, 'row', split_axis=1, concat_axis=1, tiled=True)  184 us
    psum x1, blocking collectives, body(): selected_row_sum, rhs_sum = lax.psum((chosen, rhs_part), 'row')  105 us
    psum x1, waiting for transfers between devices, body(): fitted = lax.psum(fitted_portion, 'col')  59.2 us
    split x4, local copies, waits for them, and re-layouts, body(): jnp.split(spread, lax.axis_size('row'), axis=1)  33 us
    all_to_all x1, local copies, waits for them, and re-layouts, body(): lax.all_to_all(mixed, 'row', split_axis=1, concat_axis=1, tiled=True)  19.5 us
  transfers between devices with their start and end apart: 4, of which 3 were waited for; matrix products, arithmetic and copies ran while one was open for 1% of the time, Pallas kernels for 0%

profile of v1, /device:TPU:2, one launch (start us, length us, event | category | flops | bytes accessed | tf_op | source)
XLA Modules:
  0.0 946.7 jit_solution(11927991178455147520)
XLA Ops:
  7.2 1.0 convert_element_type.14
  8.1 4.1 multiply_bitcast_fusion.1
  12.3 1.5 copy.204
  13.7 8.6 fusion.29
  22.3 18.4 %convolution_bitcast_fusion = f32[32,512,128]{2,1,0:T(8,128)} fusion(f32[32,512,128]{2,1,0:T(8,128)S(1)} %fusion.29), kind=kOutput, calls=%fused_computation.6 | convolution fusion | flops 12895649792 | bytes 16777216 | tf_op jit(solution)/shard_map/cbs,ba->cas/dot_general | solution.py:27
  40.7 9.3 reshape.47
  50.0 5.4 fusion.93
  55.4 9.3 fusion.92
  64.7 9.0 fusion.91
  73.7 9.3 fusion.90
  85.3 196.0 %all_to_all.10 = f32[64,32,1,1024]{3,1,2,0:T(8,128)S(1)} all-to-all(f32[64,32,1,1024]{3,1,2,0:T(8,128)S(1)} %constant_dynamic-update-slice_fusion), channel_id=1, replica_groups=mesh['row'=64,'col'=4] {'row'}, dimensions={0} | all-to-all | bytes 16777216 | tf_op jit(solution)/shard_map/all_to_all | solution.py:32
  281.2 12.5 %multiply_bitcast_fusion = f32[32,64,1024]{2,1,0:T(8,128)S(1)} fusion(f32[64,32,1,1024]{3,1,2,0:T(8,128)S(1)} %all_to_all.10), kind=kOutput, calls=%fused_computation.4 | convolution fusion | flops 1612840960 | bytes 16777216 | tf_op jit(solution)/shard_map/cpj,pk->ckj/dot_general | solution.py:35
  293.7 8.5 copy.136
  302.2 8.0 all-to-all-start.1
  310.4 184.1 %all-to-all-done.1 = f32[32,64,1024]{2,0,1:T(8,128)} async-done(((f32[32,64,1024]{2,0,1:T(8,128)}), f32[32,64,1024]{2,0,1:T(8,128)}, u32[]{:S(2)}, u32[]{:S(2)}) %all-to-all-start.1) | async-done | bytes 8388640 | tf_op jit(solution)/shard_map/all_to_all | solution.py:37
  494.5 19.5 %copy.137 = f32[32,64,1024]{0,2,1:T(8,128)} copy(f32[32,64,1024]{2,0,1:T(8,128)} %all-to-all-done.1) | data formatting | bytes 16777216 | tf_op jit(solution)/shard_map/all_to_all | solution.py:37
  514.0 16.0 %gather_fusion = f32[2048,32]{1,0:T(8,128)S(1)} fusion(f32[32,65536]{0,1:T(8,128)} %bitcast.318, s32[2048]{0:T(1024)S(1)} %broadcast_clamp_fusion), kind=kCustom, calls=%fused_computation | custom fusion | bytes 532480 | tf_op jit(solution)/shard_map/jit(_take)/gather | solution.py:43
  530.0 2.4 select_bitcast_fusion
  532.5 185.4 %all-reduce.4.cloned.1.call-done = f32[32,2048]{0,1:T(8,128)} async-done(((f32[32,2048]{0,1:T(8,128)}), f32[32,2048]{0,1:T(8,128)}) %all-reduce.4.cloned.1.call-update) | async-done | bytes 262160 | tf_op jit(solution)/shard_map/psum | solution.py:47
  717.9 2.2 copy.138
  720.3 0.6 dynamic-slice.1
  721.5 8.9 convolution_bitcast_fusion.1
  730.4 104.7 %psum.22 = f32[32]{0:T(128)S(1)} all-reduce(f32[32]{0:T(128)S(1)} %convolution_bitcast_fusion.1), channel_id=1, replica_groups=mesh['row'=64,'col'=4] {'row'}, use_global_device_ids=true, to_apply=%region_3.4 | all-reduce | flops 32 | bytes 256 | tf_op jit(solution)/shard_map/psum | solution.py:47
  835.3 10.7 %all-reduce = f32[128]{0:T(128)S(1)} all-reduce(f32[128]{0:T(128)S(1)} %dynamic-update-slice.3), channel_id=1, replica_groups=mesh['row'=64,'col'=4] {'col'}, use_global_device_ids=true, to_apply=%add | all-reduce | flops 128 | bytes 1024
  846.1 2.6 fusion.94
  848.7 11.7 %cholesky.16 = f32[128,128]{1,0:T(8,128)S(1)} custom-call(f32[128,128]{1,0:T(8,128)S(1)} %fusion.34), custom_call_target="Cholesky" | custom-call | tf_op jit(solution)/shard_map/jit(cholesky)/cholesky | solution.py:53
  860.5 0.6 compare_reduce_fusion
  861.1 0.7 fusion.23
  861.8 9.8 %custom-call.8 = f32[1,128,128]{1,2,0:T(8,128)S(1)} custom-call(f32[1,128,128]{2,1,0:T(8,128)S(1)} %fusion.23), custom_call_target="InvertDiagBlocksLowerTriangular" | custom-call | tf_op jit(solution)/shard_map/triangular_solve | solution.py:54
  872.0 7.1 fusion.63
  879.0 59.2 %all-reduce.6.cloned.1.call-done = f32[65536]{0:T(1024)} async-done(((f32[65536]{0:T(1024)}), f32[65536]{0:T(1024)}) %all-reduce.6.cloned.1.call-update) | async-done | bytes 262160 | tf_op jit(solution)/shard_map/psum | solution.py:63
  938.3 1.7 sub.22
  (88 shorter events, 2.7 us)
Async XLA Ops:
  302.2 8.1 copy-start.1
  302.2 192.3 %all-to-all-start.1 = ((f32[32,64,1024]{2,0,1:T(8,128)}), f32[32,64,1024]{2,0,1:T(8,128)}, u32[]{:S(2)}, u32[]{:S(2)}) async-start(f32[32,64,1024]{2,0,1:T(8,128)} %copy.136), calls=%async_computation.1 | async-start | bytes 16777216 | tf_op jit(solution)/shard_map/all_to_all | solution.py:37
  310.2 407.7 %all-reduce.4.cloned.1.call-start = ((), (), s32[]{:S(2)}) async-start(), calls=%async_computation.2 | async-start | bytes 2097152 | tf_op jit(solution)/shard_map/psum | solution.py:47
  310.4 409.9 %copy-start.3 = (u32[256]{0:T(256)S(1)}, u32[256]{0:T(256)}, u32[]{:S(2)}) copy-start(u32[256]{0:T(256)} %constant.164) | copy-start | bytes 3076
  310.4 411.1 %copy-start = (f32[65536]{0:T(1024)S(1)}, f32[65536]{0:T(1024)}, u32[]{:S(2)}) copy-start(f32[65536]{0:T(1024)} %param.7) | copy-start | bytes 786436
  532.5 313.6 %all-gather.2.cloned.1.call-start = ((), (), s32[]{:S(2)}) async-start(), calls=%async_computation.3 | async-start | bytes 1310720 | tf_op jit(solution)/shard_map/all_gather | solution.py:49
  720.2 218.1 %all-reduce.6.cloned.1.call-start = ((), (), s32[]{:S(2)}) async-start(), calls=%async_computation.4 | async-start | bytes 524288 | tf_op jit(solution)/shard_map/psum | solution.py:63
  871.8 68.2 %copy-start.2 = (f32[1,128]{1,0:T(1,128)}, f32[1,128]{1,0:T(1,128)S(1)}, u32[]{:S(2)}) copy-start(f32[1,128]{1,0:T(1,128)S(1)} %fusion.32) | copy-start | bytes 1540
Sparse Core Ops, SparseCore 0:
  532.6 185.2 all-reduce.3
  720.3 23.8 all-gather.1
  879.2 59.0 all-reduce.5
